TPU v7x, 128 devices: a whole 4x4x4 slice. The times are simulated.
128 devices in a mesh: seq: 64 (over z, y, x), exp: 2 (over core).
Axes of the slice: x: 4, y: 4, z: 4, core: 2. Of those that a mesh axis runs over, the one named last changes fastest.
Arguments:
- queries: bfloat16 [16384, 1024], P('seq', 'exp'), may hold values from -170 to 170
- keys: bfloat16 [16384, 1024], P('seq', 'exp'), may hold values from -5 to 5
- values: bfloat16 [16384, 1024], P('seq', 'exp'), may hold values from -6 to 6
- resid: bfloat16 [16384, 2048], P(('seq', 'exp')), may hold values from -6 to 6
- pair_ids: int32 [16384], replicated, may hold values from 0 to 63, never falling along the last dimension, each value on 1 to 512 neighbouring positions
- out_weight: bfloat16 [1024, 2048], P('exp'), may hold values from -0.1875 to 0.1875
- norm_gain: float32 [2048], replicated, may hold values from 0.5 to 1.5
- experts: int32 [16384, 6], P(('seq', 'exp')), may hold values from 0 to 63, all different within a row; in each aligned block of 128 rows (0 to 127, 128 to 255, ...) at most 24 rows name the same one
- gates: float32 [16384, 6], P(('seq', 'exp')), may hold values from 0.05 to 0.5
- w_gate: bfloat16 [64, 2048, 704], P('seq', None, 'exp'), may hold values from -0.125 to 0.125
- w_up: bfloat16 [64, 2048, 704], P('seq', None, 'exp'), may hold values from -0.125 to 0.125
- w_down: bfloat16 [64, 704, 2048], P('seq', 'exp'), may hold values from -0.21875 to 0.21875
Outputs:
- mixed: bfloat16 [16384, 2048], P(('seq', 'exp'))
Inputs may be any that keep to these rules, and one draw needn't show every extreme that they name: In the aligned blocks of 128 rows no expert is named more than 24 times, a bound that some block reaches; each row names 6 different experts. `pair_ids`: pair numbers never fall along the sequence; each pair has 1 to 512 tokens, one exactly that many.
All inputs are finite; a program needn't handle non-finite values.
Results may differ from a plain program's by a relative error of at most 0.012.
Values may be sent and summed in bfloat16 or wider, within the bound.
A program may use at most 128 MiB of HBM per device.

v0:
```python
import math
import jax
import jax.numpy as jnp
from jax import lax
from jax.sharding import PartitionSpec as P

HD = 128
TOP = 6


def with_halo(cells, sides, width):
    for axis, dim in sides:
        count = lax.axis_size(axis)
        ends = count - 1
        head = lax.slice_in_dim(cells, 0, width, axis=dim)
        tail = lax.slice_in_dim(cells, cells.shape[dim] - width, cells.shape[dim], axis=dim)
        cells = jnp.concatenate(
            [
                lax.ppermute(tail, axis, [(i, (i + 1) % count) for i in range(ends)]),
                cells,
                lax.ppermute(head, axis, [((i + 1) % count, i) for i in range(ends)]),
            ],
            axis=dim,
        )
    return cells


def send_back(result):
    return lax.all_to_all(result, "seq", split_axis=0, concat_axis=0, tiled=True)


def shards(
    queries,
    keys,
    values,
    resid,
    pair_ids,
    out_weight,
    norm_gain,
    experts,
    gates,
    w_gate,
    w_up,
    w_down,
):
    tok_rows = queries.shape[0]
    local_width = queries.shape[1]
    local_heads = local_width // HD
    shard = lax.axis_index("seq")
    stacked = jnp.stack([keys, values])
    widened = with_halo(stacked, (("seq", 1),), tok_rows)
    id_pad = jnp.pad(pair_ids, (tok_rows, tok_rows), constant_values=-1)
    key_ids = lax.dynamic_slice_in_dim(id_pad, shard * tok_rows, 3 * tok_rows, 0)
    query_ids = lax.dynamic_slice_in_dim(id_pad, shard * tok_rows + tok_rows, tok_rows, 0)
    query_pos = jnp.arange(tok_rows, dtype=jnp.int32) + tok_rows
    key_pos = jnp.arange(3 * tok_rows, dtype=jnp.int32)
    allowed = (query_ids[:, None] == key_ids[None, :]) & (
        jnp.abs(query_pos[:, None] - key_pos[None, :]) < tok_rows
    )
    query_heads = queries.reshape(tok_rows, local_heads, HD)
    key_heads = widened[0].reshape(3 * tok_rows, local_heads, HD)
    value_heads = widened[1].reshape(3 * tok_rows, local_heads, HD)
    score = jnp.einsum(
        "qhd,khd->hqk", query_heads, key_heads, preferred_element_type=jnp.float32
    ) / math.sqrt(HD)
    score = jnp.where(allowed[None], score, -jnp.inf)
    top = jnp.max(score, axis=-1, keepdims=True)
    weights = jnp.exp(score - top)
    probs = (weights / jnp.sum(weights, axis=-1, keepdims=True)).astype(jnp.bfloat16)
    attended = jnp.einsum("hqk,khd->qhd", probs, value_heads, preferred_element_type=jnp.float32)
    attended = attended.reshape(tok_rows, local_width).astype(jnp.bfloat16)
    moe_rows = resid.shape[0]
    projected = lax.psum(
        jnp.dot(attended, out_weight, preferred_element_type=jnp.float32).astype(jnp.bfloat16),
        "exp",
    ).astype(jnp.float32)
    projected = lax.dynamic_slice_in_dim(projected, lax.axis_index("exp") * moe_rows, moe_rows, 0)
    stream = resid.astype(jnp.float32) + projected
    meansq = jnp.mean(stream * stream, axis=-1, keepdims=True)
    normed = (stream * lax.rsqrt(meansq + 1e-05) * norm_gain).astype(jnp.bfloat16)
    n_experts = lax.axis_size("seq") * w_gate.shape[0]
    capacity = 2 * moe_rows * TOP // n_experts
    flat_experts = experts.reshape(-1)
    onehot = (flat_experts[:, None] == jnp.arange(n_experts, dtype=jnp.int32)[None, :]).astype(
        jnp.int32
    )
    ranks = jnp.cumsum(onehot, axis=0) - onehot
    slot_index = jnp.sum(ranks * onehot, axis=1)
    destination = flat_experts * capacity + slot_index
    token_of = jnp.arange(moe_rows * TOP, dtype=jnp.int32) // TOP
    outgoing = (
        jnp.zeros((n_experts * capacity, normed.shape[1]), jnp.bfloat16)
        .at[destination]
        .set(normed[token_of])
    )
    outgoing = outgoing.reshape(n_experts, capacity, normed.shape[1])
    arrived = lax.all_to_all(outgoing, "seq", split_axis=0, concat_axis=0, tiled=True)
    sources = arrived.shape[0]
    slots = arrived.shape[1]
    inputs = arrived.reshape(sources * slots, arrived.shape[2])
    group = lax.all_gather(inputs, "exp", axis=0, tiled=True)
    gate_part = jnp.dot(group, w_gate[0], preferred_element_type=jnp.float32)
    up_part = jnp.dot(group, w_up[0], preferred_element_type=jnp.float32)
    act = (jax.nn.silu(gate_part) * up_part).astype(jnp.bfloat16)
    result = lax.psum_scatter(
        jnp.dot(act, w_down[0], preferred_element_type=jnp.float32).astype(jnp.bfloat16),
        "exp",
        scatter_dimension=0,
        tiled=True,
    )
    result = result.reshape(sources, slots, result.shape[1])
    back = send_back(result)
    gathered = back.reshape(n_experts * capacity, back.shape[2])[destination]
    gathered = gathered.reshape(moe_rows, TOP, gathered.shape[1]).astype(jnp.float32)
    mixture = jnp.einsum("mk,mkd->md", gates, gathered)
    return (stream + mixture).astype(jnp.bfloat16)


def solution(mesh):
    in_specs = (
        P("seq", "exp"),
        P("seq", "exp"),
        P("seq", "exp"),
        P(("seq", "exp"), None),
        P(),
        P("exp", None),
        P(),
        P(("seq", "exp"), None),
        P(("seq", "exp"), None),
        P("seq", None, "exp"),
        P("seq", None, "exp"),
        P("seq", "exp", None),
    )
    out_specs = P(("seq", "exp"), None)
    return jax.shard_map(shards, mesh=mesh, in_specs=in_specs, out_specs=out_specs, check_vma=False)
```

profile of v0, /device:TPU:10, one launch (start us, length us, event | category | flops | bytes accessed | tf_op | source)
XLA Modules:
  0.0 383.7 jit_solution(15358219397726013312)
XLA Ops:
  6.5 1.2 copy.16
  7.8 1.1 copy.17
  8.9 3.4 collective-permute-start
  12.3 2.4 collective-permute-start.1
  14.8 0.8 pad_dynamic-slice_fusion.1
  15.6 0.8 pad_dynamic-slice_fusion
  16.4 0.3 fusion.18
  16.6 7.9 %collective-permute-done = bf16[2,256,512]{1,2,0:T(8,128)(2,1)} collective-permute-done((bf16[2,256,512]{1,2,0:T(8,128)(2,1)S(1)}, bf16[2,256,512]{1,2,0:T(8,128)(2,1)}, u32[]{:S(2)}, u32[]{:S(2)}) %collective-permute-start) | collective-permute-done | bytes 524320 | tf_op jit(solution)/shard_map/ppermute | solution.py:19
  24.6 3.1 collective-permute-done.1
  27.7 1.3 pad_maximum_fusion
  29.1 0.6 fusion.19
  29.8 1.6 fusion.32
  31.4 0.4 fusion.16
  31.8 1.7 convolution_convert_fusion.1
  34.1 1.8 reduce-window.6
  35.9 0.3 slice_reduce_fusion
  36.6 28.0 %all-reduce.3.cloned.1.call-done = bf16[256,2048]{1,0:T(8,128)(2,1)} async-done(((bf16[256,2048]{1,0:T(8,128)(2,1)}), bf16[256,2048]{1,0:T(8,128)(2,1)}) %all-reduce.3.cloned.1.call-update) | async-done | bytes 1048592 | tf_op jit(solution)/shard_map/psum | solution.py:73
  64.6 1.3 multiply_reduce_fusion
  65.9 1.3 multiply_convert_fusion
  67.2 24.2 %scatter_custom_fusion = bf16[1536,2048]{1,0:T(8,128)(2,1)} fusion(s32[768]{0:T(1024)S(1)} %fusion.26, bf16[128,2048]{1,0:T(8,128)(2,1)S(1)} %multiply_convert_fusion, s32[1024]{0:T(1024)S(1)} %pad_clamp_fusion.1, bf16[]{:T(256)} %constant.50.clone.1), kind=kCustom, calls=%fused_computation.8 | custom fusion | bytes 6291458 | tf_op jit(solution)/shard_map/scatter | solution.py:94
  91.4 84.0 %all_to_all.10 = bf16[64,24,2048]{2,1,0:T(8,128)(2,1)} all-to-all(bf16[64,24,2048]{2,1,0:T(8,128)(2,1)} %bitcast.73), channel_id=1, replica_groups=mesh['seq'=64,'exp'=2] {'seq'}, dimensions={0} | all-to-all | bytes 12582912 | tf_op jit(solution)/shard_map/all_to_all | solution.py:97
  175.4 26.4 %all-gather.2.cloned.1.call-done = bf16[3072,2048]{1,0:T(8,128)(2,1)} async-done(((bf16[1536,2048]{1,0:T(8,128)(2,1)}), bf16[3072,2048]{1,0:T(8,128)(2,1)}) %all-gather.2.cloned.1.call-update) | async-done | bytes 12582928 | tf_op jit(solution)/shard_map/all_gather | solution.py:101
  201.8 9.8 %fusion.14 = f32[3072,352]{0,1:T(8,128)} fusion(bf16[3072,2048]{1,0:T(8,128)(2,1)} %all-gather.2.cloned.1.call-done, bf16[1,2048,352]{1,2,0:T(8,128)(2,1)S(1)} %copy-done.8), kind=kOutput, calls=%fused_computation.23 | convolution fusion | flops 4429185024 | bytes 18350080 | tf_op jit(solution)/shard_map/dot_general | solution.py:102
  211.6 18.6 %convolution_convert_fusion = bf16[3072,2048]{1,0:T(8,128)(2,1)} fusion(bf16[3072,2048]{1,0:T(8,128)(2,1)} %all-gather.2.cloned.1.call-done, f32[3072,352]{0,1:T(8,128)} %fusion.14, bf16[1,352,2048]{2,1,0:T(8,128)(2,1)} %param.23, bf16[1,2048,352]{1,2,0:T(8,128)(2,1)} %param.22), kind=kOutput, calls=%fused_computation.4 | convolution fusion | flops 8871149568 | bytes 32374784 | tf_op jit(solution)/shard_map/dot_general | solution.py:106
  230.2 25.7 %reduce-scatter.2.cloned.1.call-done = bf16[1536,2048]{1,0:T(8,128)(2,1)} async-done(((bf16[3072,2048]{1,0:T(8,128)(2,1)}), bf16[1536,2048]{1,0:T(8,128)(2,1)}) %reduce-scatter.2.cloned.1.call-update) | async-done | bytes 6291472 | tf_op jit(solution)/shard_map/reduce_scatter | solution.py:105
  255.9 10.7 %all-to-all-start.1 = ((bf16[64,24,2048]{2,1,0:T(8,128)(2,1)}), bf16[64,24,2048]{2,1,0:T(8,128)(2,1)}, u32[]{:S(2)}, u32[]{:S(2)}) async-start(bf16[64,24,2048]{2,1,0:T(8,128)(2,1)} %bitcast.74), calls=%async_computation.2 | async-start | bytes 12582912 | tf_op jit(solution)/shard_map/all_to_all | solution.py:29
  266.6 0.2 copy.27
  266.8 88.4 %all-to-all-done.1 = bf16[64,24,2048]{2,1,0:T(8,128)(2,1)} async-done(((bf16[64,24,2048]{2,1,0:T(8,128)(2,1)}), bf16[64,24,2048]{2,1,0:T(8,128)(2,1)}, u32[]{:S(2)}, u32[]{:S(2)}) %all-to-all-start.1) | async-done | bytes 6291488 | tf_op jit(solution)/shard_map/all_to_all | solution.py:29
  355.2 10.8 %gather_fusion = bf16[768,2048]{1,0:T(8,128)(2,1)} fusion(bf16[1536,2048]{1,0:T(8,128)(2,1)} %bitcast.14, s32[1024]{0:T(1024)S(1)} %pad_clamp_fusion), kind=kCustom, calls=%fused_computation.1 | custom fusion | bytes 6294528 | tf_op jit(solution)/shard_map/gather | solution.py:113
  365.9 6.4 %reshape.179 = bf16[128,6,2048]{2,1,0:T(8,128)(2,1)} reshape(bf16[768,2048]{1,0:T(8,128)(2,1)} %gather_fusion) | data formatting | bytes 6291456 | tf_op jit(solution)/shard_map/reshape | solution.py:114
  372.4 3.5 fusion.33
  375.9 1.3 fusion.17
  (40 shorter events, 1.2 us)
Async XLA Ops:
  6.5 25.3 %copy-start = (bf16[512,2048]{1,0:T(8,128)(2,1)S(1)}, bf16[512,2048]{1,0:T(8,128)(2,1)}, u32[]{:S(2)}) copy-start(bf16[512,2048]{1,0:T(8,128)(2,1)} %param.17) | copy-start | bytes 6291460
  6.5 58.0 %all-reduce.3.cloned.1.call-start = ((), (), s32[]{:S(2)}) async-start(), calls=%async_computation.3 | async-start | bytes 2097152 | tf_op jit(solution)/shard_map/psum | solution.py:73
  8.9 15.7 %collective-permute-start = (bf16[2,256,512]{1,2,0:T(8,128)(2,1)S(1)}, bf16[2,256,512]{1,2,0:T(8,128)(2,1)}, u32[]{:S(2)}, u32[]{:S(2)}) collective-permute-start(bf16[2,256,512]{1,2,0:T(8,128)(2,1)S(1)} %pad_maximum_fusion.1), channel_id=1, source_target_pairs={{0,2},{2,4},{4,6},{6,8},{8,10},{10,12},{12,14},{14,16},{16,18},{18... | collective-permute-start | bytes 1572872 | tf_op jit(solution)/shard_map/ppermute | solution.py:19
  12.3 15.4 %collective-permute-start.1 = (bf16[2,256,512]{1,2,0:T(8,128)(2,1)S(1)}, bf16[2,256,512]{1,2,0:T(8,128)(2,1)}, u32[]{:S(2)}, u32[]{:S(2)}) collective-permute-start(bf16[2,256,512]{1,2,0:T(8,128)(2,1)S(1)} %pad_maximum_fusion.1), channel_id=1, source_target_pairs={{2,0},{4,2},{6,4},{8,6},{10,8},{12,10},{14,12},{16,14},{18,16},{20... | collective-permute-start | bytes 1572872 | tf_op jit(solution)/shard_map/ppermute | solution.py:21
  16.6 12.5 %copy-start.4 = (bf16[256,512]{1,0:T(8,128)(2,1)S(1)}, bf16[256,512]{1,0:T(8,128)(2,1)}, u32[]{:S(2)}) copy-start(bf16[256,512]{1,0:T(8,128)(2,1)} %param.12) | copy-start | bytes 786436
  31.8 1.9 copy-start.5
  31.8 32.8 %copy-start.2 = (bf16[128,2048]{1,0:T(8,128)(2,1)S(1)}, bf16[128,2048]{1,0:T(8,128)(2,1)}, u32[]{:S(2)}) copy-start(bf16[128,2048]{1,0:T(8,128)(2,1)} %param.15) | copy-start | bytes 1572868
  31.8 34.1 %copy-start.6 = (f32[2048]{0:T(1024)S(1)}, f32[2048]{0:T(1024)}, u32[]{:S(2)}) copy-start(f32[2048]{0:T(1024)} %param.18) | copy-start | bytes 24580
  33.6 168.2 %all-gather.2.cloned.1.call-start = ((), (), s32[]{:S(2)}) async-start(), calls=%async_computation.4 | async-start | bytes 18874368 | tf_op jit(solution)/shard_map/all_gather | solution.py:101
  175.3 26.5 %copy-start.8 = (bf16[1,2048,352]{1,2,0:T(8,128)(2,1)S(1)}, bf16[1,2048,352]{1,2,0:T(8,128)(2,1)}, u32[]{:S(2)}) copy-start(bf16[1,2048,352]{1,2,0:T(8,128)(2,1)} %param.21) | copy-start | bytes 4325380
  175.4 80.5 %reduce-scatter.2.cloned.1.call-start = ((), (), s32[]{:S(2)}) async-start(), calls=%async_computation.5 | async-start | bytes 18874368 | tf_op jit(solution)/shard_map/reduce_scatter | solution.py:105
  255.9 10.7 %copy-start.7 = (f32[128,6]{0,1:T(8,128)S(1)}, f32[128,6]{0,1:T(8,128)}, u32[]{:S(2)}) copy-start(f32[128,6]{0,1:T(8,128)} %param.20) | copy-start | bytes 9220
  255.9 99.3 %all-to-all-start.1 = ((bf16[64,24,2048]{2,1,0:T(8,128)(2,1)}), bf16[64,24,2048]{2,1,0:T(8,128)(2,1)}, u32[]{:S(2)}, u32[]{:S(2)}) async-start(bf16[64,24,2048]{2,1,0:T(8,128)(2,1)} %bitcast.74), calls=%async_computation.2 | async-start | bytes 12582912 | tf_op jit(solution)/shard_map/all_to_all | solution.py:29
  365.9 11.2 %copy-start.1 = (bf16[512,2048]{1,0:T(8,128)(2,1)S(1)}, bf16[512,2048]{1,0:T(8,128)(2,1)}, u32[]{:S(2)}) copy-start(bf16[512,2048]{1,0:T(8,128)(2,1)} %param.17) | copy-start | bytes 6291460
  372.4 3.5 copy-start.3
Sparse Core Ops, SparseCore 0:
  33.7 30.8 all-reduce.2
  175.5 26.2 all-gather.1
  230.3 25.5 reduce-scatter.1
where the time goes:
time: 384 us
  waiting for transfers between devices  180 us (47%)
  blocking collectives  84 us (22%)
  local copies, waits for them, and re-layouts  45.7 us (12%)
  matrix products  34.6 us (9%)
  starting transfers between devices  16.6 us (4%)
  between operations  13.4 us (3%)
  other arithmetic  9.89 us (3%)
    all_to_all x1, waiting for transfers between devices, send_back(): lax.all_to_all(result, 'seq', split_axis=0, concat_axis=0, tiled=True)  88.4 us
    all_to_all x1, blocking collectives, shards(): lax.all_to_all(outgoing, 'seq', split_axis=0, concat_axis=0, tiled=True)  84 us
    psum x1, waiting for transfers between devices, shards(): lax.psum(jnp.dot(attended, out_weight, preferred_element_type=jnp.float32...  28 us
    all_gather x1, waiting for transfers between devices, shards(): group = lax.all_gather(inputs, 'exp', axis=0, tiled=True)  26.4 us
    reduce_scatter x1, waiting for transfers between devices, shards(): lax.psum_scatter(jnp.dot(act, w_down[0], preferred_element_type=jnp.float...  25.7 us
    scatter x1, local copies, waits for them, and re-layouts, shards(): outgoing = jnp.zeros((n_experts * capacity, normed.shape[1]), jnp.bfloat1...  24.2 us
    dot_general x1, matrix products, shards(): jnp.dot(act, w_down[0], preferred_element_type=jnp.float32)  18.6 us
    gather x1, local copies, waits for them, and re-layouts, shards(): gathered = back.reshape(n_experts * capacity, back.shape[2])[destination]  10.8 us
  transfers between devices with their start and end apart: 6, of which 6 were waited for; matrix products, arithmetic and copies ran while one was open for 1% of the time, Pallas kernels for 0%

commit v1 on v0

--- a/solution.py
+++ b/solution.py
@@ -98,7 +98,11 @@
     sources = arrived.shape[0]
     slots = arrived.shape[1]
     inputs = arrived.reshape(sources * slots, arrived.shape[2])
-    group = lax.all_gather(inputs, "exp", axis=0, tiled=True)
+    peers = lax.axis_size("exp")
+    repeats = [peers if d == 0 else 1 for d in range(inputs.ndim)]
+    group = lax.all_to_all(
+        jnp.tile(inputs, repeats), "exp", split_axis=0, concat_axis=0, tiled=True
+    )
     gate_part = jnp.dot(group, w_gate[0], preferred_element_type=jnp.float32)
     up_part = jnp.dot(group, w_up[0], preferred_element_type=jnp.float32)
     act = (jax.nn.silu(gate_part) * up_part).astype(jnp.bfloat16)

time: 384 us -> 372 us (0.969)
  waiting for transfers between devices: 180 us -> 151 us
  blocking collectives: 84 us -> 97.8 us
  local copies, waits for them, and re-layouts: 45.7 us -> 51.7 us
    all_gather x1 -> x0, waiting for transfers between devices: 26.4 us -> none  [shards(): group = lax.all_gather(inputs, 'exp', axis=0, tiled=True)]
    all_to_all x0 -> x1, blocking collectives: none -> 14 us  [shards(): lax.all_to_all(jnp.tile(inputs, repeats), 'exp', split_axis=0, concat_axi...]
    unnamed x22 -> x24, local copies, waits for them, and re-layouts: 2.62 us -> 7.1 us
  transfers between devices with their start and end apart: 6 -> 5, of which waited for: 6 -> 5; matrix products, arithmetic and copies ran while one was open for 1% -> 1% of each run, Pallas kernels for 0% -> 0%
where the time goes in v1:
time: 372 us
  waiting for transfers between devices  151 us (41%)
  blocking collectives  97.8 us (26%)
  local copies, waits for them, and re-layouts  51.7 us (14%)
  matrix products  31.2 us (8%)
  starting transfers between devices  16.6 us (4%)
  between operations  13.7 us (4%)
  other arithmetic  9.89 us (3%)
    all_to_all x1, waiting for transfers between devices, send_back(): lax.all_to_all(result, 'seq', split_axis=0, concat_axis=0, tiled=True)  88.8 us
    all_to_all x1, blocking collectives, shards(): lax.all_to_all(outgoing, 'seq', split_axis=0, concat_axis=0, tiled=True)  83.9 us
    psum x1, waiting for transfers between devices, shards(): lax.psum(jnp.dot(attended, out_weight, preferred_element_type=jnp.float32...  28 us
    scatter x1, local copies, waits for them, and re-layouts, shards(): outgoing = jnp.zeros((n_experts * capacity, normed.shape[1]), jnp.bfloat1...  24.2 us
    reduce_scatter x1, waiting for transfers between devices, shards(): lax.psum_scatter(jnp.dot(act, w_down[0], preferred_element_type=jnp.float...  23 us
    dot_general x1, matrix products, shards(): jnp.dot(act, w_down[0], preferred_element_type=jnp.float32)  18.7 us
    all_to_all x1, blocking collectives, shards(): lax.all_to_all(jnp.tile(inputs, repeats), 'exp', split_axis=0, concat_axi...  14 us
    gather x1, local copies, waits for them, and re-layouts, shards(): gathered = back.reshape(n_experts * capacity, back.shape[2])[destination]  10.8 us
  transfers between devices with their start and end apart: 5, of which 5 were waited for; matrix products, arithmetic and copies ran while one was open for 1% of the time, Pallas kernels for 0%

profile of v1, /device:TPU:10, one launch (start us, length us, event | category | flops | bytes accessed | tf_op | source)
XLA Modules:
  0.0 371.7 jit_solution(6378567580375284651)
XLA Ops:
  6.5 1.2 copy.16
  7.8 1.1 copy.17
  8.9 3.4 collective-permute-start
  12.3 2.4 collective-permute-start.1
  14.8 0.8 pad_dynamic-slice_fusion.1
  15.6 0.8 pad_dynamic-slice_fusion
  16.6 7.9 %collective-permute-done = bf16[2,256,512]{1,2,0:T(8,128)(2,1)} collective-permute-done((bf16[2,256,512]{1,2,0:T(8,128)(2,1)S(1)}, bf16[2,256,512]{1,2,0:T(8,128)(2,1)}, u32[]{:S(2)}, u32[]{:S(2)}) %collective-permute-start) | collective-permute-done | bytes 524320 | tf_op jit(solution)/shard_map/ppermute | solution.py:19
  24.6 3.1 collective-permute-done.1
  27.7 1.3 pad_maximum_fusion
  29.1 0.6 fusion.19
  29.8 1.6 fusion.32
  31.4 0.4 fusion.16
  31.8 1.7 convolution_convert_fusion.1
  34.1 1.8 reduce-window.6
  35.9 0.3 slice_reduce_fusion
  36.6 28.0 %all-reduce.3.cloned.1.call-done = bf16[256,2048]{1,0:T(8,128)(2,1)} async-done(((bf16[256,2048]{1,0:T(8,128)(2,1)}), bf16[256,2048]{1,0:T(8,128)(2,1)}) %all-reduce.3.cloned.1.call-update) | async-done | bytes 1048592 | tf_op jit(solution)/shard_map/psum | solution.py:73
  64.6 1.3 multiply_reduce_fusion
  65.9 1.3 multiply_convert_fusion
  67.2 24.2 %scatter_custom_fusion = bf16[1536,2048]{1,0:T(8,128)(2,1)} fusion(s32[768]{0:T(1024)S(1)} %fusion.26, bf16[128,2048]{1,0:T(8,128)(2,1)S(1)} %multiply_convert_fusion, s32[1024]{0:T(1024)S(1)} %pad_clamp_fusion.1, bf16[]{:T(256)} %constant.50.clone.1), kind=kCustom, calls=%fused_computation.8 | custom fusion | bytes 6291458 | tf_op jit(solution)/shard_map/scatter | solution.py:94
  91.4 83.9 %all_to_all.19 = bf16[64,24,2048]{2,1,0:T(8,128)(2,1)S(1)} all-to-all(bf16[64,24,2048]{2,1,0:T(8,128)(2,1)} %bitcast.73), channel_id=1, replica_groups=mesh['seq'=64,'exp'=2] {'seq'}, dimensions={0} | all-to-all | bytes 12582912 | tf_op jit(solution)/shard_map/all_to_all | solution.py:97
  175.2 1.5 tile.9
  176.8 14.0 %all_to_all.20 = bf16[2,1536,2048]{2,1,0:T(8,128)(2,1)S(1)} all-to-all(bf16[2,1536,2048]{2,1,0:T(8,128)(2,1)S(1)} %tile.9), channel_id=1, replica_groups=mesh['seq'=64,'exp'=2] {'exp'}, dimensions={0} | all-to-all | bytes 25165824 | tf_op jit(solution)/shard_map/all_to_all | solution.py:103
  190.8 4.5 %copy-done.2 = bf16[2,1536,2048]{2,1,0:T(8,128)(2,1)} copy-done((bf16[2,1536,2048]{2,1,0:T(8,128)(2,1)}, bf16[2,1536,2048]{2,1,0:T(8,128)(2,1)S(1)}, u32[]{:S(2)}) %copy-start.2) | copy-done | bytes 12582936
  195.3 6.3 %fusion.14 = f32[3072,352]{0,1:T(8,128)} fusion(bf16[3072,2048]{1,0:T(8,128)(2,1)S(1)} %bitcast.75, bf16[1,2048,352]{1,2,0:T(8,128)(2,1)S(1)} %copy-done.9), kind=kOutput, calls=%fused_computation.23 | convolution fusion | flops 4429185024 | bytes 18350080 | tf_op jit(solution)/shard_map/dot_general | solution.py:106
  201.6 18.7 %convolution_convert_fusion = bf16[3072,2048]{1,0:T(8,128)(2,1)} fusion(bf16[3072,2048]{1,0:T(8,128)(2,1)} %bitcast.76, f32[3072,352]{0,1:T(8,128)} %fusion.14, bf16[1,352,2048]{2,1,0:T(8,128)(2,1)} %param.23, bf16[1,2048,352]{1,2,0:T(8,128)(2,1)} %param.22), kind=kOutput, calls=%fused_computation.4 | convolution fusion | flops 8871149568 | bytes 32374784 | tf_op jit(solution)/shard_map/dot_general | solution.py:110
  220.2 23.0 %reduce-scatter.2.cloned.1.call-done = bf16[1536,2048]{1,0:T(8,128)(2,1)} async-done(((bf16[3072,2048]{1,0:T(8,128)(2,1)}), bf16[1536,2048]{1,0:T(8,128)(2,1)}) %reduce-scatter.2.cloned.1.call-update) | async-done | bytes 6291472 | tf_op jit(solution)/shard_map/reduce_scatter | solution.py:109
  243.2 10.7 %all-to-all-start.2 = ((bf16[64,24,2048]{2,1,0:T(8,128)(2,1)}), bf16[64,24,2048]{2,1,0:T(8,128)(2,1)}, u32[]{:S(2)}, u32[]{:S(2)}) async-start(bf16[64,24,2048]{2,1,0:T(8,128)(2,1)} %bitcast.77), calls=%async_computation.3 | async-start | bytes 12582912 | tf_op jit(solution)/shard_map/all_to_all | solution.py:29
  254.1 88.8 %all-to-all-done.2 = bf16[64,24,2048]{2,1,0:T(8,128)(2,1)} async-done(((bf16[64,24,2048]{2,1,0:T(8,128)(2,1)}), bf16[64,24,2048]{2,1,0:T(8,128)(2,1)}, u32[]{:S(2)}, u32[]{:S(2)}) %all-to-all-start.2) | async-done | bytes 6291488 | tf_op jit(solution)/shard_map/all_to_all | solution.py:29
  342.9 10.8 %gather_fusion = bf16[768,2048]{1,0:T(8,128)(2,1)} fusion(bf16[1536,2048]{1,0:T(8,128)(2,1)} %bitcast.15, s32[1024]{0:T(1024)S(1)} %pad_clamp_fusion), kind=kCustom, calls=%fused_computation.1 | custom fusion | bytes 6294528 | tf_op jit(solution)/shard_map/gather | solution.py:117
  353.7 6.4 %reshape.182 = bf16[128,6,2048]{2,1,0:T(8,128)(2,1)} reshape(bf16[768,2048]{1,0:T(8,128)(2,1)} %gather_fusion) | data formatting | bytes 6291456 | tf_op jit(solution)/shard_map/reshape | solution.py:118
  360.1 3.5 fusion.33
  363.6 1.3 fusion.17
  (41 shorter events, 1.6 us)
Async XLA Ops:
  6.5 25.3 %copy-start = (bf16[512,2048]{1,0:T(8,128)(2,1)S(1)}, bf16[512,2048]{1,0:T(8,128)(2,1)}, u32[]{:S(2)}) copy-start(bf16[512,2048]{1,0:T(8,128)(2,1)} %param.17) | copy-start | bytes 6291460
  6.5 58.0 %all-reduce.3.cloned.1.call-start = ((), (), s32[]{:S(2)}) async-start(), calls=%async_computation.4 | async-start | bytes 2097152 | tf_op jit(solution)/shard_map/psum | solution.py:73
  8.9 15.7 %collective-permute-start = (bf16[2,256,512]{1,2,0:T(8,128)(2,1)S(1)}, bf16[2,256,512]{1,2,0:T(8,128)(2,1)}, u32[]{:S(2)}, u32[]{:S(2)}) collective-permute-start(bf16[2,256,512]{1,2,0:T(8,128)(2,1)S(1)} %pad_maximum_fusion.1), channel_id=1, source_target_pairs={{0,2},{2,4},{4,6},{6,8},{8,10},{10,12},{12,14},{14,16},{16,18},{18... | collective-permute-start | bytes 1572872 | tf_op jit(solution)/shard_map/ppermute | solution.py:19
  12.3 15.4 %collective-permute-start.1 = (bf16[2,256,512]{1,2,0:T(8,128)(2,1)S(1)}, bf16[2,256,512]{1,2,0:T(8,128)(2,1)}, u32[]{:S(2)}, u32[]{:S(2)}) collective-permute-start(bf16[2,256,512]{1,2,0:T(8,128)(2,1)S(1)} %pad_maximum_fusion.1), channel_id=1, source_target_pairs={{2,0},{4,2},{6,4},{8,6},{10,8},{12,10},{14,12},{16,14},{18,16},{20... | collective-permute-start | bytes 1572872 | tf_op jit(solution)/shard_map/ppermute | solution.py:21
  16.6 12.5 %copy-start.5 = (bf16[256,512]{1,0:T(8,128)(2,1)S(1)}, bf16[256,512]{1,0:T(8,128)(2,1)}, u32[]{:S(2)}) copy-start(bf16[256,512]{1,0:T(8,128)(2,1)} %param.12) | copy-start | bytes 786436
  31.8 1.9 copy-start.6
  31.8 32.8 %copy-start.3 = (bf16[128,2048]{1,0:T(8,128)(2,1)S(1)}, bf16[128,2048]{1,0:T(8,128)(2,1)}, u32[]{:S(2)}) copy-start(bf16[128,2048]{1,0:T(8,128)(2,1)} %param.15) | copy-start | bytes 1572868
  31.8 34.1 %copy-start.7 = (f32[2048]{0:T(1024)S(1)}, f32[2048]{0:T(1024)}, u32[]{:S(2)}) copy-start(f32[2048]{0:T(1024)} %param.18) | copy-start | bytes 24580
  33.6 209.7 %reduce-scatter.2.cloned.1.call-start = ((), (), s32[]{:S(2)}) async-start(), calls=%async_computation.5 | async-start | bytes 18874368 | tf_op jit(solution)/shard_map/reduce_scatter | solution.py:109
  176.8 18.5 %copy-start.9 = (bf16[1,2048,352]{1,2,0:T(8,128)(2,1)S(1)}, bf16[1,2048,352]{1,2,0:T(8,128)(2,1)}, u32[]{:S(2)}) copy-start(bf16[1,2048,352]{1,2,0:T(8,128)(2,1)} %param.21) | copy-start | bytes 4325380
  190.8 4.5 %copy-start.2 = (bf16[2,1536,2048]{2,1,0:T(8,128)(2,1)}, bf16[2,1536,2048]{2,1,0:T(8,128)(2,1)S(1)}, u32[]{:S(2)}) copy-start(bf16[2,1536,2048]{2,1,0:T(8,128)(2,1)S(1)} %all_to_all.20) | copy-start | bytes 37748740
  243.2 10.7 %copy-start.8 = (f32[128,6]{0,1:T(8,128)S(1)}, f32[128,6]{0,1:T(8,128)}, u32[]{:S(2)}) copy-start(f32[128,6]{0,1:T(8,128)} %param.20) | copy-start | bytes 9220
  243.2 99.6 %all-to-all-start.2 = ((bf16[64,24,2048]{2,1,0:T(8,128)(2,1)}), bf16[64,24,2048]{2,1,0:T(8,128)(2,1)}, u32[]{:S(2)}, u32[]{:S(2)}) async-start(bf16[64,24,2048]{2,1,0:T(8,128)(2,1)} %bitcast.77), calls=%async_computation.3 | async-start | bytes 12582912 | tf_op jit(solution)/shard_map/all_to_all | solution.py:29
  353.7 11.2 %copy-start.1 = (bf16[512,2048]{1,0:T(8,128)(2,1)S(1)}, bf16[512,2048]{1,0:T(8,128)(2,1)}, u32[]{:S(2)}) copy-start(bf16[512,2048]{1,0:T(8,128)(2,1)} %param.17) | copy-start | bytes 6291460
  360.1 3.5 copy-start.4
Sparse Core Ops, SparseCore 0:
  33.7 30.8 all-reduce.2
  220.3 22.8 reduce-scatter.1
